TPU v7x, 32 devices: a whole 2x2x4 slice. The times are simulated.
32 devices in a mesh: gx: 8 (over y, x, core), gy: 4 (over z).
Axes of the slice: x: 2, y: 2, z: 4, core: 2. Of those that a mesh axis runs over, the one named last changes fastest.
Arguments:
- tokens: bfloat16 [4096, 2048], P(('gx', 'gy')), may hold values from -6 to 6
- expert_ids: int32 [4096, 8], P(('gx', 'gy')), may hold values from 0 to 31, all different within a row; in each aligned block of 128 rows (0 to 127, 128 to 255, ...) at most 96 rows name the same one
- w_gate: bfloat16 [32, 2048, 768], P(('gx', 'gy')), may hold values from -0.125 to 0.125
- w_up: bfloat16 [32, 2048, 768], P(('gx', 'gy')), may hold values from -0.125 to 0.125
- down_error: float32 [32, 768, 2048], P(('gx', 'gy')), may hold values from -18 to 18
Outputs:
- gram_error: float32 [32, 768, 2048], P(('gx', 'gy'))
Inputs may be any that keep to these rules, and one draw needn't show every extreme that they name: `expert_ids`: among the rows of one device no expert is named more than 96 times, a bound that some block reaches; every expert is named by some row; the 8 ids of a row are distinct.
All inputs are finite; a program needn't handle non-finite values.
Results may differ from a plain program's by a relative error of at most 0.0036.
Values may be sent and summed in bfloat16 or wider, within the bound.
A program may use at most 128 MiB of HBM per device.

v0:
```python
import jax
import jax.numpy as jnp
from jax import lax
from jax.experimental import pallas as pl
from jax.experimental.pallas import tpu as pltpu
from jax.sharding import PartitionSpec as P

MESH = pl.DeviceIdType.MESH
LANES = 128


def fused_kernel(
    x_ref, wg_hbm, wu_hbm, out_ref,
    tok, wg, wu, hid, acc, cnt,
    recv, precv, s_x, s_y, s_dx, s_dy, s_p, s_up, s_dn, l_sem,
):
    gx = lax.axis_index("gx")
    z = lax.axis_index("gy")
    rows = x_ref.shape[0]
    half = rows // 2
    width = wg.shape[0]
    core = gx % 2
    px = (gx // 2) % 2
    py = gx // 4
    expert = gx * 4 + z

    def plane_of(a, b):
        return b * 2 + a

    here = plane_of(px, py)
    planes = (here, plane_of(1 - px, py), plane_of(px, 1 - py), plane_of(1 - px, 1 - py))

    def dev(a, b, c):
        return b * 4 + a * 2 + c

    x_dev = (dev(1 - px, py, core), z)
    y_dev = (dev(px, 1 - py, core), z)
    p_dev = (dev(px, py, 1 - core), z)
    up_dev = (gx, z + 1)
    dn_dev = (gx, z - 1)

    mirror = z // 2
    inner = z + (3 - 2 * z) * mirror

    def level(k):
        base = k + inner * (1 - 2 * k) * (1 - k // 2)
        return base + (3 - 2 * base) * mirror

    def block(plane, lev, c):
        return tok.at[plane, lev, pl.ds(c * rows, rows), :]

    def piece(plane, lev, h):
        return tok.at[plane, lev, pl.ds(core * rows + h * half, half), :]

    def copy(src, dst, ssem, rsem, to):
        return pltpu.make_async_remote_copy(
            src_ref=src, dst_ref=dst, send_sem=ssem, recv_sem=rsem,
            device_id=to, device_id_type=MESH,
        )

    def col_copy(k, ssem, to, src=None):
        lev = level(k)
        spot = block(here, lev, core)
        return copy(spot if src is None else src, spot, ssem.at[k], recv.at[here, lev, 0], to)

    def diag_x(k):
        lev = level(k)
        spot = piece(planes[2], lev, 0)
        return copy(spot, spot, s_dx.at[k], recv.at[planes[2], lev, 0], x_dev)

    def diag_y(k):
        lev = level(k)
        spot = piece(planes[1], lev, 1)
        return copy(spot, spot, s_dy.at[k], recv.at[planes[1], lev, 1], y_dev)

    def partner_copy(j, k, src=None):
        lev = level(k)
        spot = block(planes[j], lev, core)
        return copy(spot if src is None else src, spot, s_p.at[j, k], precv.at[planes[j], lev], p_dev)

    def wait_block(j, k):
        lev = level(k)
        spot = block(planes[j], lev, core)
        copy(spot, spot, s_p.at[j, k], recv.at[planes[j], lev, 0], p_dev).wait_recv()

    def wait_piece(j, k, h):
        lev = level(k)
        spot = piece(planes[j], lev, h)
        copy(spot, spot, s_p.at[j, k], recv.at[planes[j], lev, h], p_dev).wait_recv()

    def wait_partner(j, k):
        lev = level(k)
        spot = block(planes[j], lev, 1 - core)
        copy(spot, spot, s_p.at[j, k], precv.at[planes[j], lev], p_dev).wait_recv()

    def unit(j, k):
        wait_partner(j, k)
        lev = level(k)
        view = tok.at[planes[j], lev]
        named = view[:, pl.ds(width, LANES)].astype(jnp.float32)
        hit = jnp.max((named == expert.astype(jnp.float32)).astype(jnp.float32), axis=1, keepdims=True)
        cnt[...] += jnp.broadcast_to(jnp.sum(hit, axis=0, keepdims=True), cnt.shape)
        step = hid.shape[1] // 3

        def columns(n, carry):
            cols = pl.ds(pl.multiple_of(n * step, step), step)
            rows_in = view[:, pl.ds(0, width)]
            gate = jnp.dot(rows_in, wg[:, cols], preferred_element_type=jnp.float32)
            upward = jnp.dot(rows_in, wu[:, cols], preferred_element_type=jnp.float32)
            value = gate / (1.0 + jnp.exp(-gate)) * upward
            hid[:, cols] = jnp.where(hit > 0.5, value, 0.0).astype(jnp.bfloat16)
            return carry

        lax.fori_loop(0, 3, columns, 0)

        def bands(n, carry):
            cols = pl.ds(pl.multiple_of(n * step, step), step)
            acc[cols, :] += lax.dot_general(
                hid[:, cols], hid[...], (((0,), (0,)), ((), ())),
                preferred_element_type=jnp.float32,
            )
            return carry

        lax.fori_loop(0, 3, bands, 0)

    barrier = pltpu.get_barrier_semaphore()
    for to in (x_dev, y_dev, p_dev):
        pl.semaphore_signal(barrier, inc=1, device_id=to, device_id_type=MESH)

    @pl.when(z < 3)
    def _():
        pl.semaphore_signal(barrier, inc=1, device_id=up_dev, device_id_type=MESH)

    @pl.when(z > 0)
    def _():
        pl.semaphore_signal(barrier, inc=1, device_id=dn_dev, device_id_type=MESH)

    local = pltpu.make_async_copy(x_ref, block(here, z, core), l_sem.at[0])
    load_g = pltpu.make_async_copy(wg_hbm, wg, l_sem.at[1])
    load_u = pltpu.make_async_copy(wu_hbm, wu, l_sem.at[2])
    local.start()
    load_g.start()
    load_u.start()
    pl.semaphore_wait(barrier, 4 + inner)

    @pl.when(z < 3)
    def _():
        col_copy(0, s_up, up_dev, x_ref).start()

    @pl.when(z > 0)
    def _():
        col_copy(0, s_dn, dn_dev, x_ref).start()

    col_copy(0, s_x, x_dev, x_ref).start()
    col_copy(0, s_y, y_dev, x_ref).start()
    partner_copy(0, 0, x_ref).start()
    acc[...] = jnp.zeros_like(acc)
    cnt[...] = jnp.zeros_like(cnt)
    local.wait()
    load_g.wait()
    load_u.wait()

    def goes_up(k):
        return jnp.logical_and(level(k) < z, z < 3)

    def goes_down(k):
        return jnp.logical_and(level(k) > z, z > 0)

    def column(k):
        wait_block(0, k)

        @pl.when(goes_up(k))
        def _():
            col_copy(k, s_up, up_dev).start()

        @pl.when(goes_down(k))
        def _():
            col_copy(k, s_dn, dn_dev).start()

        col_copy(k, s_x, x_dev).start()
        col_copy(k, s_y, y_dev).start()
        partner_copy(0, k).start()

    def turn(k, carry):
        unit(0, k)
        wait_block(2, k)
        diag_x(k).start()
        wait_block(1, k)
        diag_y(k).start()
        partner_copy(1, k).start()
        partner_copy(2, k).start()

        @pl.when(k < 3)
        def _():
            column(k + 1)

        unit(1, k)
        unit(2, k)
        wait_piece(3, k, 0)
        wait_piece(3, k, 1)
        partner_copy(3, k).start()
        unit(3, k)
        return carry

    lax.fori_loop(0, 4, turn, 0)
    out_ref[...] = acc[...] / cnt[0:1, 0:1]

    @pl.when(z < 3)
    def _():
        col_copy(0, s_up, up_dev).wait_send()

    @pl.when(z > 0)
    def _():
        col_copy(0, s_dn, dn_dev).wait_send()

    def drain(k, carry):
        @pl.when(goes_up(k))
        def _():
            col_copy(k, s_up, up_dev).wait_send()

        @pl.when(goes_down(k))
        def _():
            col_copy(k, s_dn, dn_dev).wait_send()

        col_copy(k, s_x, x_dev).wait_send()
        col_copy(k, s_y, y_dev).wait_send()
        diag_x(k).wait_send()
        diag_y(k).wait_send()
        for j in range(4):
            partner_copy(j, k).wait_send()
        return carry

    lax.fori_loop(0, 4, drain, 0)


def fused_local(tokens, expert_ids, w_gate, w_up, down_error):
    rows, width = tokens.shape
    hidden = w_gate.shape[2]
    named = jnp.pad(
        expert_ids.astype(jnp.bfloat16),
        ((0, 0), (0, LANES - expert_ids.shape[1])),
        constant_values=-1.0,
    )
    packed = jnp.concatenate([tokens, named], axis=1)
    vmem = pl.BlockSpec(memory_space=pltpu.VMEM)
    hbm = pl.BlockSpec(memory_space=pltpu.HBM)
    dma = pltpu.SemaphoreType.DMA
    mean_gram = pl.pallas_call(
        fused_kernel,
        out_shape=jax.ShapeDtypeStruct((hidden, hidden), jnp.float32),
        in_specs=[vmem, hbm, hbm],
        out_specs=vmem,
        scratch_shapes=[
            pltpu.VMEM((4, 4, 2 * rows, width + LANES), jnp.bfloat16),
            pltpu.VMEM((width, hidden), jnp.bfloat16),
            pltpu.VMEM((width, hidden), jnp.bfloat16),
            pltpu.VMEM((2 * rows, hidden), jnp.bfloat16),
            pltpu.VMEM((hidden, hidden), jnp.float32),
            pltpu.VMEM((8, LANES), jnp.float32),
            dma((4, 4, 2)), dma((4, 4)),
            dma((4,)), dma((4,)), dma((4,)), dma((4,)), dma((4, 4)), dma((4,)), dma((4,)),
            dma((3,)),
        ],
        compiler_params=pltpu.CompilerParams(
            collective_id=0, has_side_effects=True, vmem_limit_bytes=56 * 1024 * 1024
        ),
    )(packed, w_gate[0], w_up[0])
    return jnp.dot(mean_gram, down_error[0], preferred_element_type=jnp.float32)[None]


def hidden_rows(received, w_gate, w_up):
    sources, slots, width = received.shape
    flat_rows = received.reshape(sources * slots, width)
    gate = jnp.dot(flat_rows, w_gate[0], preferred_element_type=jnp.float32)
    upward = jnp.dot(flat_rows, w_up[0], preferred_element_type=jnp.float32)
    hidden = (jax.nn.silu(gate) * upward).astype(jnp.bfloat16)
    return hidden.reshape(sources, slots, hidden.shape[1])


def cross_gram(first, second):
    return lax.dot_general(
        first, second, (((0,), (0,)), ((), ())), preferred_element_type=jnp.float32
    )


def gram_of(hidden):
    middle = hidden.shape[1] // 2
    left_part = hidden[:, :middle]
    right_part = hidden[:, middle:]
    upper_left = cross_gram(left_part, left_part)
    upper_right = cross_gram(left_part, right_part)
    lower_right = cross_gram(right_part, right_part)
    top_band = jnp.concatenate([upper_left, upper_right], axis=1)
    bottom_band = jnp.concatenate([upper_right.T, lower_right], axis=1)
    return jnp.concatenate([top_band, bottom_band], axis=0)


def local(tokens, expert_ids, w_gate, w_up, down_error):
    across = lax.axis_size("gx")
    within = lax.axis_size("gy")
    experts = across * within
    tok_count, top_count = expert_ids.shape
    width = tokens.shape[1]
    assigned = tok_count * top_count
    capacity = 3 * assigned // experts
    flat_ids = expert_ids.reshape(assigned)
    onehot = (flat_ids[:, None] == jnp.arange(experts, dtype=jnp.int32)[None, :]).astype(
        jnp.bfloat16
    )
    positions = jnp.arange(assigned, dtype=jnp.int32)
    lower = (positions[:, None] >= positions[None, :]).astype(jnp.bfloat16)
    running = jnp.dot(lower, onehot, preferred_element_type=jnp.float32)
    slot_of = (jnp.sum(running * onehot, axis=1) - 1.0).astype(jnp.int32)
    target = flat_ids * capacity + slot_of
    picked = tokens[positions // top_count]
    outgoing = jnp.zeros((experts * capacity, width), jnp.bfloat16).at[target].set(picked)
    tallies = jnp.sum(onehot.astype(jnp.float32), axis=0)
    loads = lax.psum_scatter(tallies, ("gx", "gy"), scatter_dimension=0, tiled=True)
    hidden = hidden_rows(
        lax.all_to_all(
            outgoing.reshape(experts, capacity, width),
            ("gx", "gy"),
            split_axis=0,
            concat_axis=0,
            tiled=True,
        ),
        w_gate,
        w_up,
    )
    hidden = hidden.reshape(experts * capacity, hidden.shape[2])
    gram = gram_of(hidden)
    mean_gram = gram / loads[0]
    product = jnp.dot(
        mean_gram,
        down_error[0],
        preferred_element_type=jnp.float32,
        precision=lax.Precision.HIGHEST,
    )
    return product[None]


def solution(mesh):
    small = mesh.shape["gx"] == 8 and mesh.shape["gy"] == 4
    return jax.shard_map(
        fused_local if small else local,
        mesh=mesh,
        in_specs=(
            P(("gx", "gy"), None),
            P(("gx", "gy"), None),
            P(("gx", "gy"), None, None),
            P(("gx", "gy"), None, None),
            P(("gx", "gy"), None, None),
        ),
        out_specs=P(("gx", "gy"), None, None),
        check_vma=False,
    )
```

profile of v0, /device:TPU:0, one launch (start us, length us, event | category | flops | bytes accessed | tf_op | source)
XLA Modules:
  0.0 107.8 jit_solution(17377745045748056899)
XLA Ops:
  0.0 0.7 convert_element_type.5
  0.7 0.1 copy.7
  0.8 1.9 %fusion.6.x_ref = bf16[128,2176]{1,0:T(8,128)(2,1)} fusion(bf16[128,8]{1,0:T(8,128)(2,1)S(1)} %copy.7, bf16[128,2048]{1,0:T(8,128)(2,1)} %param.5), kind=kLoop, calls=%fused_computation.5 | loop fusion | flops 1671168 | bytes 1083392 | tf_op jit(solution)/shard_map/concatenate | solution.py:244
  2.7 0.0 copy-start
  2.7 99.0 %shard_map.55 = f32[768,768]{1,0:T(8,128)} custom-call(bf16[128,2176]{1,0:T(8,128)(2,1)} %fusion.6.x_ref, bf16[2048,768]{1,0:T(8,128)(2,1)} %bitcast.19, bf16[2048,768]{1,0:T(8,128)(2,1)} %bitcast.20), custom_call_target="tpu_custom_call" | custom-call | tf_op jit(solution)/shard_map/pallas_call | solution.py:248
  101.7 0.0 copy-done
  101.7 6.1 %fusion.2 = f32[1,768,2048]{2,1,0:T(8,128)} fusion(f32[768,768]{1,0:T(8,128)} %shard_map.55, f32[1,768,2048]{2,1,0:T(8,128)S(1)} %copy-done), kind=kOutput, calls=%fused_computation.2 | convolution fusion | flops 2415919104 | bytes 14942208 | tf_op jit(solution)/shard_map/dot_general | solution.py:268
Async XLA Ops:
  2.7 99.0 %copy-start = (f32[1,768,2048]{2,1,0:T(8,128)S(1)}, f32[1,768,2048]{2,1,0:T(8,128)}, u32[]{:S(2)}) copy-start(f32[1,768,2048]{2,1,0:T(8,128)} %param.9) | copy-start | bytes 18874372
where the time goes:
time: 108 us
  Pallas kernels  99 us (92%)
  matrix products  6.13 us (6%)
  other arithmetic  2.58 us (2%)
    pallas_call x1, Pallas kernels, fused_local(): pl.pallas_call(fused_kernel, out_shape=jax.ShapeDtypeStruct((hidden, hidd...  99 us
    dot_general x1, matrix products, fused_local(): jnp.dot(mean_gram, down_error[0], preferred_element_type=jnp.float32)[None]  6.13 us

commit v1 on v0

--- a/solution.py
+++ b/solution.py
@@ -12,7 +12,7 @@
 def fused_kernel(
     x_ref, wg_hbm, wu_hbm, out_ref,
     tok, wg, wu, hid, acc, cnt,
-    recv, precv, s_x, s_y, s_dx, s_dy, s_p, s_up, s_dn, l_sem,
+    recv, precv, s_x, s_y, s_dx, s_dy, s_dz, s_p, s_up, s_dn, l_sem,
 ):
     gx = lax.axis_index("gx")
     z = lax.axis_index("gy")
@@ -49,44 +49,25 @@
     def block(plane, lev, c):
         return tok.at[plane, lev, pl.ds(c * rows, rows), :]
 
-    def piece(plane, lev, h):
-        return tok.at[plane, lev, pl.ds(core * rows + h * half, half), :]
-
     def copy(src, dst, ssem, rsem, to):
         return pltpu.make_async_remote_copy(
             src_ref=src, dst_ref=dst, send_sem=ssem, recv_sem=rsem,
             device_id=to, device_id_type=MESH,
         )
 
-    def col_copy(k, ssem, to, src=None):
+    def piece_copy(j, k, h, ssem, to, src=None):
         lev = level(k)
-        spot = block(here, lev, core)
-        return copy(spot if src is None else src, spot, ssem.at[k], recv.at[here, lev, 0], to)
-
-    def diag_x(k):
-        lev = level(k)
-        spot = piece(planes[2], lev, 0)
-        return copy(spot, spot, s_dx.at[k], recv.at[planes[2], lev, 0], x_dev)
-
-    def diag_y(k):
-        lev = level(k)
-        spot = piece(planes[1], lev, 1)
-        return copy(spot, spot, s_dy.at[k], recv.at[planes[1], lev, 1], y_dev)
+        spot = tok.at[planes[j], lev, pl.ds(core * rows + h * half, half), :]
+        start = spot if src is None else src.at[pl.ds(h * half, half), :]
+        return copy(start, spot, ssem, recv.at[planes[j], lev, h], to)
 
     def partner_copy(j, k, src=None):
         lev = level(k)
         spot = block(planes[j], lev, core)
         return copy(spot if src is None else src, spot, s_p.at[j, k], precv.at[planes[j], lev], p_dev)
 
-    def wait_block(j, k):
-        lev = level(k)
-        spot = block(planes[j], lev, core)
-        copy(spot, spot, s_p.at[j, k], recv.at[planes[j], lev, 0], p_dev).wait_recv()
-
     def wait_piece(j, k, h):
-        lev = level(k)
-        spot = piece(planes[j], lev, h)
-        copy(spot, spot, s_p.at[j, k], recv.at[planes[j], lev, h], p_dev).wait_recv()
+        piece_copy(j, k, h, s_x.at[k, h], p_dev).wait_recv()
 
     def wait_partner(j, k):
         lev = level(k)
@@ -143,16 +124,62 @@
     load_u.start()
     pl.semaphore_wait(barrier, 4 + inner)
 
-    @pl.when(z < 3)
-    def _():
-        col_copy(0, s_up, up_dev, x_ref).start()
-
-    @pl.when(z > 0)
-    def _():
-        col_copy(0, s_dn, dn_dev, x_ref).start()
-
-    col_copy(0, s_x, x_dev, x_ref).start()
-    col_copy(0, s_y, y_dev, x_ref).start()
+    middle = inner == 1
+    centre_dev = (gx, z + 1 - 2 * mirror)
+    outer_dev = (gx, z - 1 + 2 * mirror)
+
+    def sends_up(k):
+        return jnp.logical_and(level(k) <= z, z < 3)
+
+    def sends_down(k):
+        return jnp.logical_and(level(k) >= z, z > 0)
+
+    def along_z(k, h, act, src=None):
+        @pl.when(sends_up(k))
+        def _():
+            act(piece_copy(0, k, h, s_up.at[k, h], up_dev, src))
+
+        @pl.when(sends_down(k))
+        def _():
+            act(piece_copy(0, k, h, s_dn.at[k, h], dn_dev, src))
+
+    def start(c):
+        c.start()
+
+    def sent(c):
+        c.wait_send()
+
+    def across(k, act, src=None):
+        for h in range(2):
+            act(piece_copy(0, k, h, s_y.at[k, h], y_dev, src))
+            act(piece_copy(0, k, 1 - h, s_x.at[k, 1 - h], x_dev, src))
+
+    def diag_x(k):
+        return piece_copy(2, k, 0, s_dx.at[k], x_dev)
+
+    def diag_y(k):
+        return piece_copy(1, k, 1, s_dy.at[k], y_dev)
+
+    def diag_z(k, h, to):
+        return piece_copy(3, k, h, s_dz.at[k, h], to)
+
+    def take_column(k):
+        for h in range(2):
+            wait_piece(0, k, h)
+
+    def relay_column(k):
+        for h in range(2):
+            wait_piece(0, k, h)
+            along_z(k, h, start)
+
+    def relay_diag(k, to):
+        for h in range(2):
+            wait_piece(3, k, h)
+            diag_z(k, h, to).start()
+
+    for h in range(2):
+        along_z(0, h, start, x_ref)
+    across(0, start, x_ref)
     partner_copy(0, 0, x_ref).start()
     acc[...] = jnp.zeros_like(acc)
     cnt[...] = jnp.zeros_like(cnt)
@@ -160,72 +187,93 @@
     load_g.wait()
     load_u.wait()
 
-    def goes_up(k):
-        return jnp.logical_and(level(k) < z, z < 3)
-
-    def goes_down(k):
-        return jnp.logical_and(level(k) > z, z > 0)
-
-    def column(k):
-        wait_block(0, k)
-
-        @pl.when(goes_up(k))
-        def _():
-            col_copy(k, s_up, up_dev).start()
-
-        @pl.when(goes_down(k))
-        def _():
-            col_copy(k, s_dn, dn_dev).start()
-
-        col_copy(k, s_x, x_dev).start()
-        col_copy(k, s_y, y_dev).start()
-        partner_copy(0, k).start()
-
     def turn(k, carry):
         unit(0, k)
-        wait_block(2, k)
-        diag_x(k).start()
-        wait_block(1, k)
-        diag_y(k).start()
+
+        @pl.when(k < 2)
+        def _():
+            wait_piece(2, k, 0)
+            diag_x(k).start()
+            wait_piece(1, k, 1)
+            diag_y(k).start()
+
+        @pl.when(jnp.logical_and(k < 3, jnp.logical_not(middle)))
+        def _():
+            take_column(k + 1)
+
+        @pl.when(jnp.logical_and(k == 0, middle))
+        def _():
+            for h in range(2):
+                for n in (1, 2):
+                    wait_piece(0, n, h)
+                    along_z(n, h, start)
+
+        @pl.when(k < 3)
+        def _():
+            across(k + 1, start)
+            partner_copy(0, k + 1).start()
+
+        @pl.when(k >= 2)
+        def _():
+            wait_piece(2, k, 0)
+            wait_piece(1, k, 1)
+
+        wait_piece(2, k, 1)
+        wait_piece(1, k, 0)
         partner_copy(1, k).start()
         partner_copy(2, k).start()
-
-        @pl.when(k < 3)
-        def _():
-            column(k + 1)
-
         unit(1, k)
+
+        @pl.when(jnp.logical_and(k < 2, middle))
+        def _():
+            relay_diag(k, centre_dev)
+
+        @pl.when(jnp.logical_and(k == 1, middle))
+        def _():
+            relay_diag(2, outer_dev)
+
+        @pl.when(jnp.logical_and(k == 2, middle))
+        def _():
+            relay_diag(3, outer_dev)
+
+        @pl.when(middle)
+        def _():
+            partner_copy(3, k).start()
+
         unit(2, k)
-        wait_piece(3, k, 0)
-        wait_piece(3, k, 1)
-        partner_copy(3, k).start()
+
+        @pl.when(jnp.logical_not(middle))
+        def _():
+            wait_piece(3, k, 0)
+            wait_piece(3, k, 1)
+            partner_copy(3, k).start()
+
         unit(3, k)
+
+        @pl.when(jnp.logical_and(k == 0, middle))
+        def _():
+            relay_column(3)
+
         return carry
 
     lax.fori_loop(0, 4, turn, 0)
     out_ref[...] = acc[...] / cnt[0:1, 0:1]
 
-    @pl.when(z < 3)
-    def _():
-        col_copy(0, s_up, up_dev).wait_send()
-
-    @pl.when(z > 0)
-    def _():
-        col_copy(0, s_dn, dn_dev).wait_send()
-
     def drain(k, carry):
-        @pl.when(goes_up(k))
-        def _():
-            col_copy(k, s_up, up_dev).wait_send()
-
-        @pl.when(goes_down(k))
-        def _():
-            col_copy(k, s_dn, dn_dev).wait_send()
-
-        col_copy(k, s_x, x_dev).wait_send()
-        col_copy(k, s_y, y_dev).wait_send()
-        diag_x(k).wait_send()
-        diag_y(k).wait_send()
+        for h in range(2):
+            along_z(k, h, sent)
+        across(k, sent)
+
+        @pl.when(k < 2)
+        def _():
+            diag_x(k).wait_send()
+            diag_y(k).wait_send()
+
+        @pl.when(middle)
+        def _():
+            for h in range(2):
+                diag_z(k, h, outer_dev).wait_send()
+
         for j in range(4):
             partner_copy(j, k).wait_send()
         return carry
@@ -258,7 +306,8 @@
             pltpu.VMEM((hidden, hidden), jnp.float32),
             pltpu.VMEM((8, LANES), jnp.float32),
             dma((4, 4, 2)), dma((4, 4)),
-            dma((4,)), dma((4,)), dma((4,)), dma((4,)), dma((4, 4)), dma((4,)), dma((4,)),
+            dma((4, 2)), dma((4, 2)), dma((4,)), dma((4,)), dma((4, 2)),
+            dma((4, 4)), dma((4, 2)), dma((4, 2)),
             dma((3,)),
         ],
         compiler_params=pltpu.CompilerParams(

time: 108 us -> 97.5 us (0.903)
  Pallas kernels: 99 us -> 88.4 us
    pallas_call x1, Pallas kernels: 99 us -> 88.4 us  [fused_local(): pl.pallas_call(fused_kernel, out_shape=jax.ShapeDtypeStruct((hidden, hidd...]
where the time goes in v1:
time: 97.5 us; the launch traced here: 97.3 us
  Pallas kernels  88.4 us (91%)
  matrix products  6.13 us (6%)
  other arithmetic  2.58 us (3%)
    pallas_call x1, Pallas kernels, fused_local(): pl.pallas_call(fused_kernel, out_shape=jax.ShapeDtypeStruct((hidden, hidd...  88.4 us
    dot_general x1, matrix products, fused_local(): jnp.dot(mean_gram, down_error[0], preferred_element_type=jnp.float32)[None]  6.13 us

profile of v1, /device:TPU:0, one launch (start us, length us, event | category | flops | bytes accessed | tf_op | source)
XLA Modules:
  0.0 97.3 jit_solution(5022854481504135301)
XLA Ops:
  0.0 0.7 convert_element_type.5
  0.7 0.1 copy.7
  0.8 1.9 %fusion.6.x_ref = bf16[128,2176]{1,0:T(8,128)(2,1)} fusion(bf16[128,8]{1,0:T(8,128)(2,1)S(1)} %copy.7, bf16[128,2048]{1,0:T(8,128)(2,1)} %param.5), kind=kLoop, calls=%fused_computation.5 | loop fusion | flops 1671168 | bytes 1083392 | tf_op jit(solution)/shard_map/concatenate | solution.py:292
  2.7 0.0 copy-start
  2.7 88.4 %shard_map.55 = f32[768,768]{1,0:T(8,128)} custom-call(bf16[128,2176]{1,0:T(8,128)(2,1)} %fusion.6.x_ref, bf16[2048,768]{1,0:T(8,128)(2,1)} %bitcast.19, bf16[2048,768]{1,0:T(8,128)(2,1)} %bitcast.20), custom_call_target="tpu_custom_call" | custom-call | tf_op jit(solution)/shard_map/pallas_call | solution.py:296
  91.1 0.0 copy-done
  91.1 6.1 %fusion.2 = f32[1,768,2048]{2,1,0:T(8,128)} fusion(f32[768,768]{1,0:T(8,128)} %shard_map.55, f32[1,768,2048]{2,1,0:T(8,128)S(1)} %copy-done), kind=kOutput, calls=%fused_computation.2 | convolution fusion | flops 2415919104 | bytes 14942208 | tf_op jit(solution)/shard_map/dot_general | solution.py:317
Async XLA Ops:
  2.7 88.4 %copy-start = (f32[1,768,2048]{2,1,0:T(8,128)S(1)}, f32[1,768,2048]{2,1,0:T(8,128)}, u32[]{:S(2)}) copy-start(f32[1,768,2048]{2,1,0:T(8,128)} %param.9) | copy-start | bytes 18874372

commit v2 on v1

--- a/solution.py
+++ b/solution.py
@@ -81,28 +81,24 @@
         named = view[:, pl.ds(width, LANES)].astype(jnp.float32)
         hit = jnp.max((named == expert.astype(jnp.float32)).astype(jnp.float32), axis=1, keepdims=True)
         cnt[...] += jnp.broadcast_to(jnp.sum(hit, axis=0, keepdims=True), cnt.shape)
-        step = hid.shape[1] // 3
-
-        def columns(n, carry):
-            cols = pl.ds(pl.multiple_of(n * step, step), step)
-            rows_in = view[:, pl.ds(0, width)]
+        rows_in = view[:, pl.ds(0, width)]
+        for n in range(bands):
+            cols = pl.ds(n * step, step)
             gate = jnp.dot(rows_in, wg[:, cols], preferred_element_type=jnp.float32)
             upward = jnp.dot(rows_in, wu[:, cols], preferred_element_type=jnp.float32)
             value = gate / (1.0 + jnp.exp(-gate)) * upward
-            hid[:, cols] = jnp.where(hit > 0.5, value, 0.0).astype(jnp.bfloat16)
-            return carry
-
-        lax.fori_loop(0, 3, columns, 0)
-
-        def bands(n, carry):
-            cols = pl.ds(pl.multiple_of(n * step, step), step)
-            acc[cols, :] += lax.dot_general(
-                hid[:, cols], hid[...], (((0,), (0,)), ((), ())),
+            hid[pl.ds((j % 2) * 2 * rows, 2 * rows), cols] = jnp.where(hit > 0.5, value, 0.0).astype(jnp.bfloat16)
+
+    bands = 3
+    step = hid.shape[1] // bands
+
+    def gram():
+        for n in range(bands):
+            rest = pl.ds(n * step, hid.shape[1] - n * step)
+            acc[pl.ds(n * step, step), rest] += lax.dot_general(
+                hid[:, pl.ds(n * step, step)], hid[:, rest], (((0,), (0,)), ((), ())),
                 preferred_element_type=jnp.float32,
             )
-            return carry
-
-        lax.fori_loop(0, 3, bands, 0)
 
     barrier = pltpu.get_barrier_semaphore()
     for to in (x_dev, y_dev, p_dev):
@@ -223,6 +219,7 @@
         partner_copy(1, k).start()
         partner_copy(2, k).start()
         unit(1, k)
+        gram()
 
         @pl.when(jnp.logical_and(k < 2, middle))
         def _():
@@ -249,6 +246,7 @@
             partner_copy(3, k).start()
 
         unit(3, k)
+        gram()
 
         @pl.when(jnp.logical_and(k == 0, middle))
         def _():
@@ -257,7 +255,13 @@
         return carry
 
     lax.fori_loop(0, 4, turn, 0)
-    out_ref[...] = acc[...] / cnt[0:1, 0:1]
+    count = cnt[0:1, 0:1]
+    for n in range(bands):
+        for m in range(n, bands):
+            part = acc[pl.ds(n * step, step), pl.ds(m * step, step)] / count
+            out_ref[pl.ds(n * step, step), pl.ds(m * step, step)] = part
+            if m > n:
+                out_ref[pl.ds(m * step, step), pl.ds(n * step, step)] = part.T
 
     def drain(k, carry):
         for h in range(2):
@@ -302,7 +306,7 @@
             pltpu.VMEM((4, 4, 2 * rows, width + LANES), jnp.bfloat16),
             pltpu.VMEM((width, hidden), jnp.bfloat16),
             pltpu.VMEM((width, hidden), jnp.bfloat16),
-            pltpu.VMEM((2 * rows, hidden), jnp.bfloat16),
+            pltpu.VMEM((4 * rows, hidden), jnp.bfloat16),
             pltpu.VMEM((hidden, hidden), jnp.float32),
             pltpu.VMEM((8, LANES), jnp.float32),
             dma((4, 4, 2)), dma((4, 4)),

time: 97.5 us -> 88.5 us (0.908)
  Pallas kernels: 88.4 us -> 79.4 us
    pallas_call x1, Pallas kernels: 88.4 us -> 79.4 us  [fused_local(): pl.pallas_call(fused_kernel, out_shape=jax.ShapeDtypeStruct((hidden, hidd...]
where the time goes in v2:
time: 88.5 us; the launch traced here: 88.3 us
  Pallas kernels  79.4 us (90%)
  matrix products  6.13 us (7%)
  other arithmetic  2.58 us (3%)
    pallas_call x1, Pallas kernels, fused_local(): pl.pallas_call(fused_kernel, out_shape=jax.ShapeDtypeStruct((hidden, hidd...  79.4 us
    dot_general x1, matrix products, fused_local(): jnp.dot(mean_gram, down_error[0], preferred_element_type=jnp.float32)[None]  6.13 us
    concatenate x1, other arithmetic, fused_local(): packed = jnp.concatenate([tokens, named], axis=1)  1.89 us

profile of v2, /device:TPU:0, one launch (start us, length us, event | category | flops | bytes accessed | tf_op | source)
XLA Modules:
  0.0 88.3 jit_solution(11556262605469609757)
XLA Ops:
  0.0 0.7 convert_element_type.5
  0.7 0.1 copy.7
  0.8 1.9 %fusion.6.x_ref = bf16[128,2176]{1,0:T(8,128)(2,1)} fusion(bf16[128,8]{1,0:T(8,128)(2,1)S(1)} %copy.7, bf16[128,2048]{1,0:T(8,128)(2,1)} %param.5), kind=kLoop, calls=%fused_computation.5 | loop fusion | flops 1671168 | bytes 1083392 | tf_op jit(solution)/shard_map/concatenate | solution.py:296
  2.7 0.0 copy-start
  2.7 79.4 %shard_map.55 = f32[768,768]{1,0:T(8,128)} custom-call(bf16[128,2176]{1,0:T(8,128)(2,1)} %fusion.6.x_ref, bf16[2048,768]{1,0:T(8,128)(2,1)} %bitcast.19, bf16[2048,768]{1,0:T(8,128)(2,1)} %bitcast.20), custom_call_target="tpu_custom_call" | custom-call | tf_op jit(solution)/shard_map/pallas_call | solution.py:300
  82.2 0.0 copy-done
  82.2 6.1 %fusion.2 = f32[1,768,2048]{2,1,0:T(8,128)} fusion(f32[768,768]{1,0:T(8,128)} %shard_map.55, f32[1,768,2048]{2,1,0:T(8,128)S(1)} %copy-done), kind=kOutput, calls=%fused_computation.2 | convolution fusion | flops 2415919104 | bytes 14942208 | tf_op jit(solution)/shard_map/dot_general | solution.py:321
Async XLA Ops:
  2.7 79.5 %copy-start = (f32[1,768,2048]{2,1,0:T(8,128)S(1)}, f32[1,768,2048]{2,1,0:T(8,128)}, u32[]{:S(2)}) copy-start(f32[1,768,2048]{2,1,0:T(8,128)} %param.9) | copy-start | bytes 18874372
